TPU v7x, 32 devices: a whole 2x2x4 slice. The times are simulated.
32 devices in a mesh: seq: 8 (over y, x, core), vid: 4 (over z).
Axes of the slice: x: 2, y: 2, z: 4, core: 2. Of those that a mesh axis runs over, the one named last changes fastest.
Arguments:
- tokens: bfloat16 [32768, 768], P(('vid', 'seq')), parts along dimension 0, may hold values from -100 to 100
- latents: bfloat16 [2048, 768], P(('vid', 'seq')), parts along dimension 0, may hold values from -6 to 6
- read_weights: bfloat16 [4, 768, 768], P(None, 'seq'), may hold values from -1 to 1
- later_weights: bfloat16 [8, 768, 768], P(None, 'seq'), may hold values from -1 to 1
- head_scale: float32 [3, 12], replicated, may hold values from 1 to 40
Outputs:
- tokens_out: bfloat16 [32768, 768], P(('vid', 'seq')), parts along dimension 0
- latents_out: float32 [2048, 768], P(('vid', 'seq')), parts along dimension 0
There are 4 independent parts, one for each index of `vid`. A program takes and returns all parts, laid end to end along the dimension named above; an argument that names none is the same for every part. Nothing has to cross between parts.
All inputs are finite; a program needn't handle non-finite values.
Results may differ from a plain program's by a relative error of at most 0.01.
The roundings to bfloat16 on the way count: a program that leaves them out, or rounds other values in their place, can miss the bound.
Values may be sent and summed in bfloat16 or wider, within the bound.
A program may use at most 64 MiB of HBM per device.

v0:
```python
import functools
import math

import jax
import jax.numpy as jnp
from jax import lax
from jax.experimental import pallas as pl
from jax.experimental.pallas import tpu as pltpu
from jax.sharding import PartitionSpec as P

HEADS = 12
LANES = 128
epsilon = 1e-06
LOG2E = math.log2(math.e)
BF16 = jnp.bfloat16
F32 = jnp.float32


def rms(values):
    return values * lax.rsqrt(jnp.mean(values * values, axis=-1, keepdims=True) + epsilon)


def dot(left, right):
    return jnp.dot(left, right, preferred_element_type=F32)


def inner(left, right):
    return lax.dot_general(left, right, (((1,), (1,)), ((), ())), preferred_element_type=F32)


def group_matrix(head_dim):
    size = 2 * LANES
    row = lax.broadcasted_iota(jnp.int32, (size, size), 0) // head_dim
    col = lax.broadcasted_iota(jnp.int32, (size, size), 1) // head_dim
    return jnp.where(row == col, 1.0 / head_dim, 0.0).astype(BF16)


def head_norm(values, group):
    size = group.shape[0]
    parts = []
    for start in range(0, values.shape[1], size):
        block = values[:, start : start + size]
        square = block * block
        high = square.astype(BF16)
        low = (square - high.astype(F32)).astype(BF16)
        mean = dot(high, group) + dot(low, group)
        parts.append((block * lax.rsqrt(mean + epsilon)).astype(BF16))
    return jnp.concatenate(parts, axis=1)


def by_rows(rows, chunk, body):
    chunk = min(chunk, rows)

    def step(index, carry):
        body(pl.ds(pl.multiple_of(index * chunk, chunk), chunk))
        return carry

    lax.fori_loop(0, rows // chunk, step, 0)


def half_masks(head_dim):
    lane = lax.broadcasted_iota(jnp.int32, (1, LANES), 1) // head_dim
    return [(lane == part).astype(F32).astype(BF16) for part in range(LANES // head_dim)]


def merge_halves(parts, head_dim):
    lane = lax.broadcasted_iota(jnp.int32, parts[0].shape, 1) // head_dim
    result = parts[0]
    for part in range(1, len(parts)):
        result = jnp.where(lane == part, parts[part], result)
    return result


def attention(q_ref, k_ref, v_ref, scale_ref, which, out_ref, stats_ref, chunk, hooks=None):
    rows, width = q_ref.shape
    head_dim = width // HEADS
    per_block = LANES // head_dim
    chunk = min(chunk, rows)
    n_chunks = rows // chunk
    masks = half_masks(head_dim)
    root = 1.0 / math.sqrt(head_dim)

    def step(index, carry):
        for when, action in (hooks or {}).items():
            pl.when(index == when)(action)
        block = index // n_chunks
        part = index % n_chunks
        cols = pl.ds(pl.multiple_of(block * LANES, LANES), LANES)
        here = pl.ds(pl.multiple_of(part * chunk, chunk), chunk)
        q = q_ref[here, cols]
        k = k_ref[:, cols]
        v = v_ref[:, cols]
        results = []
        for half in range(per_block):
            head = block * per_block + half
            factor = scale_ref[which, head] * root
            scores = inner(q * masks[half], k)
            top = jnp.max(scores, axis=1, keepdims=True)
            exp_scores = jnp.exp2((scores - top) * (factor * LOG2E))
            total = jnp.sum(exp_scores, axis=1, keepdims=True)
            weights = exp_scores.astype(BF16)
            if stats_ref is not None:
                lane = lax.broadcasted_iota(jnp.int32, (chunk, LANES), 1)
                old = stats_ref[here, :]
                old = jnp.where(lane == head, top * factor, old)
                stats_ref[here, :] = jnp.where(lane == head + LANES // 2, total, old)
            mixed = dot(weights, v)
            results.append(mixed / total if stats_ref is None else mixed)
        out_ref[here, cols] = merge_halves(results, head_dim).astype(BF16)
        return carry

    lax.fori_loop(0, (width // LANES) * n_chunks, step, 0)


def read_body(tok_ref, lat_ref, w_ref, scale_ref, parts_ref, stats_ref, q_ref, k_ref, v_ref):
    group = group_matrix(tok_ref.shape[1] // HEADS)

    stats_ref[...] = jnp.zeros(stats_ref.shape, F32)

    def latent_rows(here):
        normed = rms(lat_ref[here, :].astype(F32)).astype(BF16)
        q_ref[here, :] = head_norm(dot(normed, w_ref[0]), group)

    def token_rows(here):
        normed = rms(tok_ref[here, :].astype(F32)).astype(BF16)
        k_ref[here, :] = head_norm(dot(normed, w_ref[1]), group)
        v_ref[here, :] = dot(normed, w_ref[2]).astype(BF16)

    by_rows(lat_ref.shape[0], 256, latent_rows)
    by_rows(tok_ref.shape[0], 256, token_rows)
    attention(q_ref, k_ref, v_ref, scale_ref, 0, parts_ref, stats_ref, 256)


def combine(got, stats, lat_ref, out_w_ref, w_refs, one_ref, q_ref, kv_ref):
    count = len(got)
    rows, width = got[0].shape
    head_dim = width // HEADS
    group = group_matrix(head_dim)
    per_block = LANES // head_dim
    best = functools.reduce(jnp.maximum, stats)
    rescale = [jnp.exp(item - best) for item in stats]
    half = LANES // 2
    bottom = sum(rescale[b][:, :half] * stats[b][:, half:] for b in range(count))
    inverse = 1.0 / bottom
    mixed = []
    for block in range(width // LANES):
        cols = slice(block * LANES, block * LANES + LANES)
        total = jnp.zeros((rows, LANES), F32)
        heads = range(block * per_block, block * per_block + per_block)

        def spread(values):
            return merge_halves(
                [jnp.broadcast_to(values[:, h : h + 1], (rows, LANES)) for h in heads], head_dim
            )

        for b in range(count):
            total += got[b][:, cols].astype(F32) * spread(rescale[b])
        mixed.append((total * spread(inverse)).astype(BF16))
    read_mix = jnp.concatenate(mixed, axis=1)
    lat_one = lat_ref[...].astype(F32) + dot(read_mix, out_w_ref[...])
    one_ref[...] = lat_one
    normed = rms(lat_one).astype(BF16)
    q_ref[...] = head_norm(dot(normed, w_refs[0][...]), group)
    kv_ref[:, :width] = head_norm(dot(normed, w_refs[1][...]), group)
    kv_ref[:, width:] = dot(normed, w_refs[2][...]).astype(BF16)


def combine_body(got_ref, stats_ref, lat_ref, out_w_ref, w_ref, one_ref, q_ref, kv_ref):
    count = got_ref.shape[0]
    combine(
        [got_ref[b] for b in range(count)],
        [stats_ref[b] for b in range(count)],
        lat_ref, out_w_ref, [w_ref.at[i] for i in range(3)], one_ref, q_ref, kv_ref,
    )


def self_body(one_ref, q_ref, kv_ref, w_ref, scale_ref, out_ref, in_ref, mix_ref):
    width = one_ref.shape[1]
    attention(
        q_ref, kv_ref.at[:, :width], kv_ref.at[:, width:], scale_ref, 1, mix_ref, None, 64
    )
    latents_out = one_ref[...] + dot(mix_ref[...], w_ref[...])
    out_ref[...] = latents_out
    in_ref[...] = rms(latents_out).astype(BF16)


def write_body(tok_ref, in_ref, w_ref, scale_ref, out_ref, q_ref, k_ref, v_ref, mix_ref):
    group = group_matrix(tok_ref.shape[1] // HEADS)

    def latent_rows(here):
        k_ref[here, :] = head_norm(dot(in_ref[here, :], w_ref[1]), group)
        v_ref[here, :] = dot(in_ref[here, :], w_ref[2]).astype(BF16)

    def token_rows(here):
        normed = rms(tok_ref[here, :].astype(F32)).astype(BF16)
        q_ref[here, :] = head_norm(dot(normed, w_ref[0]), group)

    def out_rows(here):
        out_ref[here, :] = (
            tok_ref[here, :].astype(F32) + dot(mix_ref[here, :], w_ref[3])
        ).astype(out_ref.dtype)

    by_rows(in_ref.shape[0], 256, latent_rows)
    by_rows(tok_ref.shape[0], 256, token_rows)
    attention(q_ref, k_ref, v_ref, scale_ref, 2, mix_ref, None, 256)
    by_rows(tok_ref.shape[0], 256, out_rows)


VM = pl.BlockSpec(memory_space=pltpu.VMEM)
SM = pl.BlockSpec(memory_space=pltpu.SMEM)


def call(body, in_specs, outs, scratch, *args):
    return pl.pallas_call(
        body,
        out_shape=[jax.ShapeDtypeStruct(shape, dtype) for shape, dtype in outs],
        in_specs=in_specs,
        out_specs=[VM] * len(outs),
        scratch_shapes=[pltpu.VMEM(shape, dtype) for shape, dtype in scratch],
        compiler_params=pltpu.CompilerParams(vmem_limit_bytes=56 * 1024 * 1024),
    )(*args)


def gathered(count, tokens, latents, read_weights, later_weights, head_scale):
    own, width = latents.shape
    rows = own * count
    slab = tokens.shape[0]
    read_full = lax.all_gather(read_weights, "seq", axis=1, tiled=True)
    later_full = lax.all_gather(later_weights, "seq", axis=1, tiled=True)
    lat_all = lax.all_gather(latents, "seq", axis=0, tiled=True)
    parts, stats = call(
        read_body,
        [VM, VM, VM, SM],
        [((rows, width), BF16), ((rows, LANES), F32)],
        [((rows, width), BF16), ((slab, width), BF16), ((slab, width), BF16)],
        tokens, lat_all, read_full[:3], head_scale,
    )
    got_parts = lax.all_to_all(
        parts.reshape(count, own, width), "seq", split_axis=0, concat_axis=0, tiled=True
    )
    got_stats = lax.all_to_all(
        stats.reshape(count, own, LANES), "seq", split_axis=0, concat_axis=0, tiled=True
    )
    lat_one, self_q, self_kv = call(
        combine_body,
        [VM] * 5,
        [((own, width), F32), ((own, width), BF16), ((own, 2 * width), BF16)],
        [],
        got_parts, got_stats, latents, read_full[3], later_full[:3],
    )
    all_kv = lax.all_gather(self_kv, "seq", axis=0, tiled=True)
    latents_out, write_in = call(
        self_body,
        [VM, VM, VM, VM, SM],
        [((own, width), F32), ((own, width), BF16)],
        [((own, width), BF16)],
        lat_one, self_q, all_kv, later_full[3], head_scale,
    )
    write_all = lax.all_gather(write_in, "seq", axis=0, tiled=True)
    (tokens_out,) = call(
        write_body,
        [VM, VM, VM, SM],
        [((slab, width), BF16)],
        [((slab, width), BF16), ((rows, width), BF16), ((rows, width), BF16), ((slab, width), BF16)],
        tokens, write_all, later_full[4:], head_scale,
    )
    return tokens_out, latents_out


class Gather:
    def __init__(self, source, place, rows, sems, item, spots, pair=None):
        send, recv = sems
        me, core, along_x, along_y, diagonal = spots
        self.done = set()
        self.paired = pair is not None

        def copy(kind, src, dst, target):
            return pltpu.make_async_remote_copy(
                src_ref=src,
                dst_ref=dst,
                send_sem=send.at[item, kind],
                recv_sem=recv.at[item, kind],
                device_id=target,
                device_id_type=pl.DeviceIdType.MESH,
            )

        unit = rows // 3 if self.paired else rows // 2
        base = pair[0] * unit if self.paired else 0

        def block(owner, start=0, size=rows):
            return place(pl.ds(pl.multiple_of(owner * rows + start, unit), size))

        def both(owner, start, size):
            return block(owner, start, size), block(owner, start, size)

        x_dev, y_dev, core_dev = {"seq": along_x}, {"seq": along_y}, {"seq": core}
        mine = source if source is not None else block(me)
        share = block(me, base, 2 * unit)
        if source is None:
            part = share
        else:
            part = source.at[pl.ds(pl.multiple_of(base, unit), 2 * unit)]
        self.first = [
            copy(0, part, share, x_dev),
            copy(1, part, share, y_dev),
            copy(2, mine, block(me), core_dev),
        ]
        self.relay = [
            copy(3, *both(along_x, base, unit), y_dev),
            copy(4, *both(along_y, base + unit, unit), x_dev),
        ]
        self.forward = [
            copy(5 + i, *both(owner, 0, rows), core_dev)
            for i, owner in enumerate((along_x, along_y, diagonal))
        ]
        self.swap = []
        if self.paired:
            self.swap = [
                copy(8 + i, *both(owner, pair[0] * 2 * unit, unit), {"vid": pair[1]})
                for i, owner in enumerate((along_x, along_y, diagonal))
            ]
        self.local = None
        if source is not None:
            self.local = pltpu.make_async_copy(source, block(me), send.at[item, 11])

    def once(self, stage):
        fresh = stage not in self.done
        self.done.add(stage)
        return fresh

    def start(self):
        if self.once("start"):
            for copy in self.first:
                copy.start()
            if self.local is not None:
                self.local.start()

    def spread(self):
        if self.once("spread"):
            onward = self.swap if self.paired else self.forward
            for i in range(2):
                self.first[i].wait_recv()
                self.relay[i].start()
                onward[i].start()

    def close(self):
        if self.once("close"):
            self.relay[0].wait_recv()
            self.relay[1].wait_recv()
            (self.swap if self.paired else self.forward)[2].start()

    def settle(self):
        if self.paired and self.once("settle"):
            for i in range(3):
                self.swap[i].wait_recv()
                self.forward[i].start()

    def need(self):
        self.spread()
        self.close()
        self.settle()
        self.first[2].wait_recv()
        for copy in self.forward:
            copy.wait_recv()
        if self.local is not None:
            self.local.wait()

    def drain(self):
        for copy in self.first + self.relay + self.forward + self.swap:
            copy.wait_send()


def whole_body(
    count, tok_ref, lat_ref, rw_ref, lw_ref, scale_ref, out_ref, lat_out_ref,
    w_ref, norm_ref, lat_all, q_ref, k_ref, v_ref, parts_ref, stats_ref,
    got_ref, got_stats, one_ref, self_q, kv_ref, mix_small, in_ref,
    wq_ref, wk_ref, wv_ref, mix_ref, send, recv, slab_send, slab_recv,
):
    me = lax.axis_index("seq")
    core = me + 1 - 2 * (me % 2)
    along_x = me + 2 - 4 * ((me // 2) % 2)
    along_y = me + 4 - 8 * (me // 4)
    diagonal = along_x + 4 - 8 * (me // 4)
    spots = (me, core, along_x, along_y, diagonal)
    own, width = lat_ref.shape
    n_read = rw_ref.shape[0]
    shard = rw_ref.shape[1]
    group = group_matrix(width // HEADS)
    sems = (send, recv)

    barrier = pltpu.get_barrier_semaphore()
    for step in range(1, count):
        pl.semaphore_signal(
            barrier, inc=1, device_id={"seq": (me + step) % count},
            device_id_type=pl.DeviceIdType.MESH,
        )
    plane = lax.axis_index("vid")
    pair = (plane % 2, plane + 1 - 2 * (plane % 2))
    pl.semaphore_signal(
        barrier, inc=1, device_id={"vid": pair[1]}, device_id_type=pl.DeviceIdType.MESH
    )
    pl.semaphore_wait(barrier, count)

    def matrix(item, index):
        source = rw_ref.at[index] if index < n_read else lw_ref.at[index - n_read]
        return Gather(source, lambda rows: w_ref.at[index, rows], shard, sems, item, spots, pair)

    def array(item, source, ref):
        return Gather(source, lambda rows: ref.at[rows], own, sems, item, spots)

    r1, r2 = matrix(0, 1), matrix(1, 2)
    lat = array(2, lat_ref, lat_all)
    r0, l4, r3 = matrix(3, 0), matrix(4, n_read + 4), matrix(5, 3)
    l0, l1, l2 = (matrix(6 + i, n_read + i) for i in range(3))
    l3, l5, l6, l7 = (matrix(9 + i, n_read + j) for i, j in enumerate((3, 5, 6, 7)))
    kv, into = array(13, None, kv_ref), array(14, None, in_ref)

    r1.start()
    r2.start()
    lat.start()
    r0.start()

    def norm_rows(here):
        norm_ref[here, :] = rms(tok_ref[here, :].astype(F32)).astype(BF16)

    slab = tok_ref.shape[0]
    by_rows(slab, 256, norm_rows)
    stats_ref[...] = jnp.zeros(stats_ref.shape, F32)
    r1.spread()
    l4.start()
    r1.close()
    r2.spread()
    r3.start()
    r2.close()
    r1.need()

    def key_rows(here):
        k_ref[here, :] = head_norm(dot(norm_ref[here, :], w_ref[1]), group)

    by_rows(slab, 256, key_rows)
    lat.spread()
    l0.start()
    r2.need()

    def value_rows(here):
        v_ref[here, :] = dot(norm_ref[here, :], w_ref[2]).astype(BF16)

    by_rows(slab, 256, value_rows)
    lat.close()
    r0.spread()
    l1.start()
    r0.close()
    l4.spread()
    lat.need()
    r0.need()
    l4.close()

    def query_rows(here):
        normed = rms(lat_all[here, :].astype(F32)).astype(BF16)
        q_ref[here, :] = head_norm(dot(normed, w_ref[0]), group)

    by_rows(lat_all.shape[0], 256, query_rows)

    def run(*actions):
        def body():
            for action in actions:
                action()

        return body

    sums = []

    def exchange(src, dst, cols, kind):
        copies = []
        for step in range(1, count):
            target = (me + step) % count
            rows = pl.ds(pl.multiple_of(target * own, own), own)
            copies.append(
                pltpu.make_async_remote_copy(
                    src_ref=src.at[rows, cols],
                    dst_ref=dst.at[step - 1, :, cols],
                    send_sem=slab_send.at[step - 1, kind],
                    recv_sem=slab_recv.at[step - 1, kind],
                    device_id={"seq": target},
                    device_id_type=pl.DeviceIdType.MESH,
                )
            )
        sums.extend(copies)

        def body():
            for copy in copies:
                copy.start()

        return body

    third = width // 3
    groups = [
        exchange(parts_ref, got_ref, slice(i * third, i * third + third), i) for i in range(3)
    ]
    attention(
        q_ref, k_ref, v_ref, scale_ref, 0, parts_ref, stats_ref, lat_all.shape[0] // 2,
        {
            0: run(l4.settle, r3.spread, l2.start),
            2: run(r3.close, l0.spread, l3.start),
            4: run(groups[0], r3.settle, l0.close, l1.spread, l5.start),
            6: run(l0.settle, l1.close, l2.spread, l6.start),
            8: run(groups[1], l1.settle, l2.close, l3.spread, l7.start),
            10: run(l2.settle, l3.close, l5.spread),
        },
    )
    groups[2]()
    exchange(stats_ref, got_stats, slice(0, LANES), 3)()
    l3.settle()
    l5.close()
    l6.spread()
    l4.need()

    def write_query_rows(here):
        wq_ref[here, :] = head_norm(dot(norm_ref[here, :], w_ref[n_read + 4]), group)

    by_rows(slab, 256, write_query_rows)
    l5.settle()
    l6.close()
    l7.spread()
    for item in (r3, l0, l1, l2):
        item.need()
    for copy in sums:
        copy.wait_recv()
    mine = pl.ds(pl.multiple_of(me * own, own), own)
    combine(
        [parts_ref[mine, :]] + [got_ref[b] for b in range(count - 1)],
        [stats_ref[mine, :]] + [got_stats[b] for b in range(count - 1)],
        lat_ref, w_ref.at[3], [w_ref.at[n_read + i] for i in range(3)],
        one_ref, self_q, kv_ref.at[mine],
    )
    kv.start()
    l6.settle()
    l7.close()
    kv.need()
    attention(
        self_q, kv_ref.at[:, :width], kv_ref.at[:, width:], scale_ref, 1, mix_small, None, own
    )
    l3.need()
    latents_out = one_ref[...] + dot(mix_small[...], w_ref[n_read + 3])
    lat_out_ref[...] = latents_out
    in_ref[mine, :] = rms(latents_out).astype(BF16)
    into.start()
    l7.settle()
    into.need()
    l5.need()

    def write_key_rows(here):
        wk_ref[here, :] = head_norm(dot(in_ref[here, :], w_ref[n_read + 5]), group)

    def write_value_rows(here):
        wv_ref[here, :] = dot(in_ref[here, :], w_ref[n_read + 6]).astype(BF16)

    by_rows(lat_all.shape[0], 256, write_key_rows)
    l6.need()
    by_rows(lat_all.shape[0], 256, write_value_rows)
    attention(
        wq_ref, wk_ref, wv_ref, scale_ref, 2, mix_ref, None, 256
    )
    l7.need()

    def out_rows(here):
        out_ref[here, :] = (
            tok_ref[here, :].astype(F32) + dot(mix_ref[here, :], w_ref[n_read + 7])
        ).astype(out_ref.dtype)

    by_rows(slab, 256, out_rows)
    for item in (r1, r2, lat, r0, l4, r3, l0, l1, l2, l3, l5, l6, l7, kv, into):
        item.drain()
    for copy in sums:
        copy.wait_send()


def cube(count, tokens, latents, read_weights, later_weights, head_scale):
    own, width = latents.shape
    rows = own * count
    slab = tokens.shape[0]
    matrices = read_weights.shape[0] + later_weights.shape[0]
    vmem = lambda *shape: pltpu.VMEM(shape, BF16)
    full = lambda *shape: pltpu.VMEM(shape, F32)
    return pl.pallas_call(
        functools.partial(whole_body, count),
        out_shape=[
            jax.ShapeDtypeStruct(tokens.shape, BF16),
            jax.ShapeDtypeStruct(latents.shape, F32),
        ],
        in_specs=[VM, VM, pl.BlockSpec(memory_space=pl.ANY), pl.BlockSpec(memory_space=pl.ANY), SM],
        out_specs=[VM, VM],
        scratch_shapes=[
            vmem(matrices, width, width),
            vmem(slab, width),
            vmem(rows, width),
            vmem(rows, width),
            vmem(slab, width),
            vmem(slab, width),
            vmem(rows, width),
            full(rows, LANES),
            vmem(count - 1, own, width),
            full(count - 1, own, LANES),
            full(own, width),
            vmem(own, width),
            vmem(rows, 2 * width),
            vmem(own, width),
            vmem(rows, width),
            vmem(slab, width),
            vmem(rows, width),
            vmem(rows, width),
            vmem(slab, width),
            pltpu.SemaphoreType.DMA((matrices + 3, 12)),
            pltpu.SemaphoreType.DMA((matrices + 3, 11)),
            pltpu.SemaphoreType.DMA((count - 1, 4)),
            pltpu.SemaphoreType.DMA((count - 1, 4)),
        ],
        compiler_params=pltpu.CompilerParams(
            vmem_limit_bytes=60 * 1024 * 1024, collective_id=0, has_side_effects=True
        ),
    )(tokens, latents, read_weights, later_weights, head_scale)


def solution(mesh):
    placed = (
        P(("vid", "seq"), None),
        P(("vid", "seq"), None),
        P(None, "seq", None),
        P(None, "seq", None),
        P(),
    )
    count = mesh.shape["seq"]
    form = cube if count == 2**3 and mesh.shape["vid"] % 2 == 0 else gathered
    return jax.shard_map(
        functools.partial(form, count),
        mesh=mesh,
        in_specs=placed,
        out_specs=(P(("vid", "seq"), None), P(("vid", "seq"), None)),
        check_vma=False,
    )
```

profile of v0, /device:TPU:1, one launch (start us, length us, event | category | flops | bytes accessed | tf_op | source)
XLA Modules:
  0.0 128.4 jit_solution(3257452206749638278)
XLA Ops:
  0.6 124.4 %shard_map.68 = (bf16[1024,768]{1,0:T(8,128)(2,1)}, f32[64,768]{1,0:T(8,128)}) custom-call(bf16[1024,768]{1,0:T(8,128)(2,1)} %tok_ref.1, bf16[64,768]{1,0:T(8,128)(2,1)} %lat_ref.1, bf16[4,96,768]{2,1,0:T(8,128)(2,1)} %rw_ref.1, bf16[8,96,768]{2,1,0:T(8,128)(2,1)} %lw_ref.1, f32[3,12]{1,0:T(4,128)} %scale_ref.1), custom_call_target="tpu_custom_call" | custom-call | tf_op jit(solution)/shard_map/pallas_call | solution.py:585
  125.0 0.0 copy-start
  125.1 2.7 %copy.9 = bf16[1024,768]{1,0:T(8,128)(2,1)} copy(bf16[1024,768]{1,0:T(8,128)(2,1)} %get-tuple-element.4) | data formatting | bytes 3145728
  127.7 0.0 copy-done
  127.8 0.7 copy.10
Async XLA Ops:
  125.0 2.7 %copy-start = (f32[64,768]{1,0:T(8,128)S(1)}, f32[64,768]{1,0:T(8,128)}, u32[]{:S(2)}) copy-start(f32[64,768]{1,0:T(8,128)} %get-tuple-element.5) | copy-start | bytes 589828
where the time goes:
time: 129 us; the launch traced here: 128 us
  Pallas kernels  124 us (96%)
  local copies, waits for them, and re-layouts  3.37 us (3%)
    pallas_call x1, Pallas kernels, cube(): pl.pallas_call(functools.partial(whole_body, count), out_shape=[jax.Shape...  124 us
    unnamed x4, local copies, waits for them, and re-layouts  3.37 us

commit v1 on v0

v1 whole, which is shorter than its diff:
```python
import functools
import math

import jax
import jax.numpy as jnp
from jax import lax
from jax.experimental import pallas as pl
from jax.experimental.pallas import tpu as pltpu
from jax.sharding import PartitionSpec as P

HEADS = 12
LANES = 128
epsilon = 1e-06
LOG2E = math.log2(math.e)
BF16 = jnp.bfloat16
F32 = jnp.float32


def rms(values):
    return values * lax.rsqrt(jnp.mean(values * values, axis=-1, keepdims=True) + epsilon)


def dot(left, right):
    return jnp.dot(left, right, preferred_element_type=F32)


def inner(left, right):
    return lax.dot_general(left, right, (((1,), (1,)), ((), ())), preferred_element_type=F32)


def group_matrix(head_dim):
    size = 2 * LANES
    row = lax.broadcasted_iota(jnp.int32, (size, size), 0) // head_dim
    col = lax.broadcasted_iota(jnp.int32, (size, size), 1) // head_dim
    return jnp.where(row == col, 1.0 / head_dim, 0.0).astype(BF16)


def head_norm(values, group):
    size = group.shape[0]
    parts = []
    for start in range(0, values.shape[1], size):
        block = values[:, start : start + size]
        square = block * block
        high = square.astype(BF16)
        low = (square - high.astype(F32)).astype(BF16)
        mean = dot(high, group) + dot(low, group)
        parts.append((block * lax.rsqrt(mean + epsilon)).astype(BF16))
    return jnp.concatenate(parts, axis=1)


def by_rows(rows, chunk, body):
    chunk = min(chunk, rows)

    def step(index, carry):
        body(pl.ds(pl.multiple_of(index * chunk, chunk), chunk))
        return carry

    lax.fori_loop(0, rows // chunk, step, 0)


def half_masks(head_dim):
    lane = lax.broadcasted_iota(jnp.int32, (1, LANES), 1) // head_dim
    return [(lane == part).astype(F32).astype(BF16) for part in range(LANES // head_dim)]


def merge_halves(parts, head_dim):
    lane = lax.broadcasted_iota(jnp.int32, parts[0].shape, 1) // head_dim
    result = parts[0]
    for part in range(1, len(parts)):
        result = jnp.where(lane == part, parts[part], result)
    return result


def attention(q_ref, k_ref, v_ref, scale_ref, which, out_ref, stats_ref, chunk, hooks=None):
    rows, width = q_ref.shape
    head_dim = width // HEADS
    per_block = LANES // head_dim
    chunk = min(chunk, rows)
    n_chunks = rows // chunk
    masks = half_masks(head_dim)
    root = 1.0 / math.sqrt(head_dim)

    def step(index, carry):
        for when, action in (hooks or {}).items():
            pl.when(index == when)(action)
        block = index // n_chunks
        part = index % n_chunks
        cols = pl.ds(pl.multiple_of(block * LANES, LANES), LANES)
        here = pl.ds(pl.multiple_of(part * chunk, chunk), chunk)
        q = q_ref[here, cols]
        k = k_ref[:, cols]
        v = v_ref[:, cols]
        results = []
        for half in range(per_block):
            head = block * per_block + half
            factor = scale_ref[which, head] * root
            scores = inner(q * masks[half], k)
            top = jnp.max(scores, axis=1, keepdims=True)
            exp_scores = jnp.exp2((scores - top) * (factor * LOG2E))
            total = jnp.sum(exp_scores, axis=1, keepdims=True)
            weights = exp_scores.astype(BF16)
            if stats_ref is not None:
                lane = lax.broadcasted_iota(jnp.int32, (chunk, LANES), 1)
                old = stats_ref[here, :]
                old = jnp.where(lane == head, top * factor, old)
                stats_ref[here, :] = jnp.where(lane == head + LANES // 2, total, old)
            mixed = dot(weights, v)
            results.append(mixed / total if stats_ref is None else mixed)
        out_ref[here, cols] = merge_halves(results, head_dim).astype(BF16)
        return carry

    lax.fori_loop(0, (width // LANES) * n_chunks, step, 0)


def read_body(tok_ref, lat_ref, w_ref, scale_ref, parts_ref, stats_ref, q_ref, k_ref, v_ref):
    group = group_matrix(tok_ref.shape[1] // HEADS)

    stats_ref[...] = jnp.zeros(stats_ref.shape, F32)

    def latent_rows(here):
        normed = rms(lat_ref[here, :].astype(F32)).astype(BF16)
        q_ref[here, :] = head_norm(dot(normed, w_ref[0]), group)

    def token_rows(here):
        normed = rms(tok_ref[here, :].astype(F32)).astype(BF16)
        k_ref[here, :] = head_norm(dot(normed, w_ref[1]), group)
        v_ref[here, :] = dot(normed, w_ref[2]).astype(BF16)

    by_rows(lat_ref.shape[0], 256, latent_rows)
    by_rows(tok_ref.shape[0], 256, token_rows)
    attention(q_ref, k_ref, v_ref, scale_ref, 0, parts_ref, stats_ref, 256)


def combine(got, stats, lat_ref, out_w_ref, w_refs, one_ref, q_ref, kv_ref):
    count = len(got)
    rows, width = got[0].shape
    head_dim = width // HEADS
    group = group_matrix(head_dim)
    per_block = LANES // head_dim
    best = functools.reduce(jnp.maximum, stats)
    rescale = [jnp.exp(item - best) for item in stats]
    half = LANES // 2
    bottom = sum(rescale[b][:, :half] * stats[b][:, half:] for b in range(count))
    inverse = 1.0 / bottom
    mixed = []
    for block in range(width // LANES):
        cols = slice(block * LANES, block * LANES + LANES)
        total = jnp.zeros((rows, LANES), F32)
        heads = range(block * per_block, block * per_block + per_block)

        def spread(values):
            return merge_halves(
                [jnp.broadcast_to(values[:, h : h + 1], (rows, LANES)) for h in heads], head_dim
            )

        for b in range(count):
            total += got[b][:, cols].astype(F32) * spread(rescale[b])
        mixed.append((total * spread(inverse)).astype(BF16))
    read_mix = jnp.concatenate(mixed, axis=1)
    lat_one = lat_ref[...].astype(F32) + dot(read_mix, out_w_ref[...])
    one_ref[...] = lat_one
    normed = rms(lat_one).astype(BF16)
    q_ref[...] = head_norm(dot(normed, w_refs[0][...]), group)
    kv_ref[:, :width] = head_norm(dot(normed, w_refs[1][...]), group)
    kv_ref[:, width:] = dot(normed, w_refs[2][...]).astype(BF16)


def combine_body(got_ref, stats_ref, lat_ref, out_w_ref, w_ref, one_ref, q_ref, kv_ref):
    count = got_ref.shape[0]
    combine(
        [got_ref[b] for b in range(count)],
        [stats_ref[b] for b in range(count)],
        lat_ref, out_w_ref, [w_ref.at[i] for i in range(3)], one_ref, q_ref, kv_ref,
    )


def self_body(one_ref, q_ref, kv_ref, w_ref, scale_ref, out_ref, in_ref, mix_ref):
    width = one_ref.shape[1]
    attention(
        q_ref, kv_ref.at[:, :width], kv_ref.at[:, width:], scale_ref, 1, mix_ref, None, 64
    )
    latents_out = one_ref[...] + dot(mix_ref[...], w_ref[...])
    out_ref[...] = latents_out
    in_ref[...] = rms(latents_out).astype(BF16)


def write_body(tok_ref, in_ref, w_ref, scale_ref, out_ref, q_ref, k_ref, v_ref, mix_ref):
    group = group_matrix(tok_ref.shape[1] // HEADS)

    def latent_rows(here):
        k_ref[here, :] = head_norm(dot(in_ref[here, :], w_ref[1]), group)
        v_ref[here, :] = dot(in_ref[here, :], w_ref[2]).astype(BF16)

    def token_rows(here):
        normed = rms(tok_ref[here, :].astype(F32)).astype(BF16)
        q_ref[here, :] = head_norm(dot(normed, w_ref[0]), group)

    def out_rows(here):
        out_ref[here, :] = (
            tok_ref[here, :].astype(F32) + dot(mix_ref[here, :], w_ref[3])
        ).astype(out_ref.dtype)

    by_rows(in_ref.shape[0], 256, latent_rows)
    by_rows(tok_ref.shape[0], 256, token_rows)
    attention(q_ref, k_ref, v_ref, scale_ref, 2, mix_ref, None, 256)
    by_rows(tok_ref.shape[0], 256, out_rows)


VM = pl.BlockSpec(memory_space=pltpu.VMEM)
SM = pl.BlockSpec(memory_space=pltpu.SMEM)


def call(body, in_specs, outs, scratch, *args):
    return pl.pallas_call(
        body,
        out_shape=[jax.ShapeDtypeStruct(shape, dtype) for shape, dtype in outs],
        in_specs=in_specs,
        out_specs=[VM] * len(outs),
        scratch_shapes=[pltpu.VMEM(shape, dtype) for shape, dtype in scratch],
        compiler_params=pltpu.CompilerParams(vmem_limit_bytes=56 * 1024 * 1024),
    )(*args)


def gathered(count, tokens, latents, read_weights, later_weights, head_scale):
    own, width = latents.shape
    rows = own * count
    slab = tokens.shape[0]
    read_full = lax.all_gather(read_weights, "seq", axis=1, tiled=True)
    later_full = lax.all_gather(later_weights, "seq", axis=1, tiled=True)
    lat_all = lax.all_gather(latents, "seq", axis=0, tiled=True)
    parts, stats = call(
        read_body,
        [VM, VM, VM, SM],
        [((rows, width), BF16), ((rows, LANES), F32)],
        [((rows, width), BF16), ((slab, width), BF16), ((slab, width), BF16)],
        tokens, lat_all, read_full[:3], head_scale,
    )
    got_parts = lax.all_to_all(
        parts.reshape(count, own, width), "seq", split_axis=0, concat_axis=0, tiled=True
    )
    got_stats = lax.all_to_all(
        stats.reshape(count, own, LANES), "seq", split_axis=0, concat_axis=0, tiled=True
    )
    lat_one, self_q, self_kv = call(
        combine_body,
        [VM] * 5,
        [((own, width), F32), ((own, width), BF16), ((own, 2 * width), BF16)],
        [],
        got_parts, got_stats, latents, read_full[3], later_full[:3],
    )
    all_kv = lax.all_gather(self_kv, "seq", axis=0, tiled=True)
    latents_out, write_in = call(
        self_body,
        [VM, VM, VM, VM, SM],
        [((own, width), F32), ((own, width), BF16)],
        [((own, width), BF16)],
        lat_one, self_q, all_kv, later_full[3], head_scale,
    )
    write_all = lax.all_gather(write_in, "seq", axis=0, tiled=True)
    (tokens_out,) = call(
        write_body,
        [VM, VM, VM, SM],
        [((slab, width), BF16)],
        [((slab, width), BF16), ((rows, width), BF16), ((rows, width), BF16), ((slab, width), BF16)],
        tokens, write_all, later_full[4:], head_scale,
    )
    return tokens_out, latents_out


MESH = pl.DeviceIdType.MESH


class Net:
    def __init__(self, send, recv):
        self.send, self.recv = send, recv
        self.count = 0
        self.sent = []

    def remote(self, src, dst, target):
        item = self.count
        self.count += 1
        copy = pltpu.make_async_remote_copy(
            src_ref=src, dst_ref=dst, send_sem=self.send.at[item], recv_sem=self.recv.at[item],
            device_id=target, device_id_type=MESH,
        )
        self.sent.append(copy)
        return copy

    def local(self, src, dst):
        item = self.count
        self.count += 1
        return pltpu.make_async_copy(src, dst, self.send.at[item])


def once(method):
    @functools.wraps(method)
    def guarded(self):
        if method.__name__ not in self.done:
            self.done.add(method.__name__)
            method(self)

    return guarded


class Place:
    def __init__(self):
        me = lax.axis_index("seq")
        plane = lax.axis_index("vid")
        self.me, self.core, self.chip = me, me % 2, me // 2
        chip = self.chip
        chip_x = chip + 1 - 2 * (chip % 2)
        chip_y = chip + 2 - 4 * (chip // 2)
        self.chips = (chip_x, chip_y, chip_x + 2 - 4 * (chip // 2))
        self.partner = {"seq": me + 1 - 2 * self.core}
        self.peers = [{"seq": 2 * other + self.core} for other in self.chips]
        self.side = plane % 2
        self.opposite = {"vid": plane + 1 - 2 * self.side}


class Weight:
    def __init__(self, net, spot, buffer, cols, pieces, shard, half, whole=False, lean=None):
        self.done = set()
        own = pl.ds(pl.multiple_of(spot.me * shard, shard), shard)
        self.local, self.near = [], []
        for source, offset, size, start in pieces:
            if whole:
                self.local.append(net.local(source, buffer.at[own]))
                self.near.append(net.remote(source, buffer.at[own], spot.partner))
                continue

            def part(core):
                return source.at[:, pl.ds(pl.multiple_of(core * half + offset, LANES), size)]

            target = buffer.at[own, start : start + size]
            self.local.append(net.local(part(spot.core), target))
            self.near.append(net.remote(part(1 - spot.core), target, spot.partner))
        if whole:
            cols = pl.ds(pl.multiple_of(spot.core * half, LANES), half)
        rows = 2 * shard
        chip_x, chip_y, diagonal = spot.chips
        to_x, to_y, _ = spot.peers

        def send(owner, start, size, target):
            block = buffer.at[pl.ds(pl.multiple_of(owner * rows + start, size), size), cols]
            return net.remote(block, block, target)

        to_x_part, to_y_part = spot.side * shard, (1 - spot.side) * shard
        self.first = [
            send(spot.chip, to_x_part, shard, to_x), send(spot.chip, to_y_part, shard, to_y)
        ]
        self.relay = [
            send(chip_x, to_x_part, shard, to_y) if lean != 1 else None,
            send(chip_y, to_y_part, shard, to_x) if lean != 0 else None,
        ]
        self.swap = [
            send(chip_x, to_x_part, shard, spot.opposite),
            send(chip_y, to_y_part, shard, spot.opposite),
        ]
        self.late = []
        self.kept = [0, 1]
        if lean is not None:
            self.kept = [lean]
            part = (to_x_part, to_y_part)[lean]
            self.late = [send(diagonal, part, shard, spot.opposite)]
        self.forward = []
        if whole:
            self.forward = [send(owner, 0, rows, spot.partner) for owner in spot.chips]

    @once
    def fetch(self):
        for copy in self.local + self.near:
            copy.start()

    @once
    def start(self):
        for copy in self.local:
            copy.wait()
        for copy in self.near:
            copy.wait_recv()
        for copy in self.first:
            copy.start()

    @once
    def spread(self):
        for i in range(2):
            self.first[i].wait_recv()
            if i in self.kept:
                self.relay[i].start()
            self.swap[i].start()

    @once
    def close(self):
        self.spread()
        for i in self.kept if self.late else ():
            self.relay[i].wait_recv()
            self.late[0].start()

    @once
    def settle(self):
        self.close()
        for i in self.kept if not self.late else ():
            self.relay[i].wait_recv()
        for copy in self.swap + self.late:
            copy.wait_recv()
        for copy in self.forward:
            copy.start()

    @once
    def need(self):
        self.settle()
        for copy in self.forward:
            copy.wait_recv()


class Rows:
    def __init__(self, net, spot, source, buffer, rows):
        self.done = set()
        to_x, to_y, _ = spot.peers
        half = rows // 2

        def block(owner, start=0, size=rows):
            return buffer.at[pl.ds(pl.multiple_of(owner * rows + start, half), size)]

        def send(owner, start, size, target):
            return net.remote(block(owner, start, size), block(owner, start, size), target)

        owners = [2 * chip + spot.core for chip in spot.chips]
        self.local = net.local(source, block(spot.me))
        self.first = [net.remote(source, block(spot.me), to) for to in (to_x, to_y, spot.partner)]
        self.relay = [send(owners[0], 0, half, to_y), send(owners[1], half, half, to_x)]
        self.forward = [send(owner, 0, rows, spot.partner) for owner in owners]

    @once
    def start(self):
        for copy in self.first:
            copy.start()
        self.local.start()

    @once
    def spread(self):
        for i in range(2):
            self.first[i].wait_recv()
            self.relay[i].start()
            self.forward[i].start()

    @once
    def close(self):
        for copy in self.relay:
            copy.wait_recv()
        self.forward[2].start()

    @once
    def need(self):
        self.spread()
        self.close()
        self.first[2].wait_recv()
        for copy in self.forward:
            copy.wait_recv()
        self.local.wait()


def unit_norm(values, group, gain=None):
    parts = []
    for start in range(0, values.shape[1], group.shape[0]):
        block = values[:, start : start + group.shape[0]]
        size = block.shape[1]
        mean = dot((block * block).astype(BF16), group[:size, :size])
        scaled = block * lax.rsqrt(mean + epsilon)
        if gain is not None:
            scaled = scaled * gain[:, start : start + size]
        parts.append(scaled.astype(BF16))
    return parts[0] if len(parts) == 1 else jnp.concatenate(parts, axis=1)


def head_gain(scale_ref, which, first, heads, head_dim):
    lane = lax.broadcasted_iota(jnp.int32, (1, heads * head_dim), 1) // head_dim
    gain = jnp.zeros(lane.shape, F32)
    for head in range(heads):
        factor = scale_ref[which, first + head] * (LOG2E / math.sqrt(head_dim))
        gain = jnp.where(lane == head, factor, gain)
    return gain


def low_half(shape):
    return lax.broadcasted_iota(jnp.int32, shape, 1) < LANES // 2


def with_ones(values):
    low = low_half((values.shape[0], LANES))
    parts = []
    for start in range(0, values.shape[1], LANES):
        block = values[:, start : start + LANES]
        parts += [jnp.where(low, block, 1.0).astype(BF16), jnp.where(low, 1.0, block).astype(BF16)]
    return jnp.concatenate(parts, axis=1)


def two_heads(q, k, values, first, second, masks):
    first[...] = inner(q * masks[0], k)
    second[...] = inner(q * masks[1], k)
    tops, sums = [], []
    for scores_ref, value in zip((first, second), values):
        scores = scores_ref[...]
        top = jnp.max(scores, axis=1, keepdims=True)
        tops.append(top)
        sums.append(dot(jnp.exp2(scores - top).astype(BF16), value))
    return tops, sums


def quotient(sums):
    low = low_half(sums[0].shape)
    mixed = jnp.where(low, sums[0], sums[1])
    total = pltpu.roll(jnp.where(low, sums[1], sums[0]), LANES // 2, 1)
    return (mixed / total).astype(BF16)


def whole_body(
    count, tok_ref, lat_ref, rw_ref, lw_ref, scale_ref, out_ref, lat_out_ref,
    norm_ref, kvq_ref, w4_ref, wself_ref, wkv_ref, full_ref, lat_all, q_ref, k_ref, va_ref,
    wide_a, wide_b, tall_a, tall_b, parts_ref, stat_ref, got_ref, got_stat, mix_all, one_ref,
    in_ref, sq_ref, sk_ref, sva_ref, att_ref, wq_ref, wk_ref, wva_ref, mix_ref, power_ref, send, recv,
):
    spot = Place()
    net = Net(send, recv)
    own, width = lat_ref.shape
    slab = tok_ref.shape[0]
    rows = own * count
    shard = rw_ref.shape[1]
    half = width // 2
    head_dim = width // HEADS
    heads = HEADS // 2
    blocks = half // LANES
    chip_rows = 2 * own
    group = group_matrix(head_dim)
    masks = half_masks(head_dim)

    barrier = pltpu.get_barrier_semaphore()
    friends = [spot.partner, spot.opposite] + spot.peers
    for friend in friends:
        pl.semaphore_signal(barrier, inc=1, device_id=friend, device_id_type=MESH)
    pl.semaphore_wait(barrier, len(friends))

    def cols(block):
        return pl.ds(pl.multiple_of(spot.core * half + block * LANES, LANES), LANES)

    def chip_block(chip):
        return pl.ds(pl.multiple_of(chip * chip_rows, chip_rows), chip_rows)

    def weight(buffer, start, size, pieces, whole=False, lean=None):
        cut = slice(start, start + size)
        return Weight(net, spot, buffer, cut, pieces, shard, half, whole, lean)

    read = [rw_ref.at[i] for i in range(4)]
    later = [lw_ref.at[i] for i in range(8)]
    kvq = [
        weight(
            kvq_ref.at[j], 0, 3 * LANES,
            [(read[m], j * LANES, LANES, i * LANES) for i, m in enumerate((1, 2, 0))],
        )
        for j in range(blocks)
    ]
    l4 = weight(w4_ref, 0, half, [(later[4], 0, half, 0)])
    l0, l1, l2 = (
        weight(wself_ref, i * half, half, [(later[i], 0, half, i * half)])
        for i in range(3)
    )
    l5, l6 = (
        weight(wkv_ref, i * half, half, [(later[5 + i], 0, half, i * half)]) for i in range(2)
    )
    r3, l3, l7 = (
        weight(full_ref.at[i], 0, half, [(source, 0, half, 0)], True)
        for i, source in enumerate((read[3], later[3], later[7]))
    )
    lat = Rows(net, spot, lat_ref, lat_all, own)
    order = kvq + [l4, r3, l0, l1, l2, l3, l5, l6, l7]

    def go(spread=(), start=()):
        for index in spread:
            order[index].spread()
        for index in start:
            order[index].start()

    lat.start()
    kvq[0].fetch()
    piece = slab // 4
    token_copies = []
    for i in range(4):
        here = pl.ds(i * piece, piece)
        norm_ref[here, :] = rms(tok_ref[here, :].astype(F32)).astype(BF16)
        copy = net.remote(
            norm_ref.at[here], norm_ref.at[pl.ds(slab + i * piece, piece)], spot.partner
        )
        copy.start()
        token_copies.append(copy)
        if i == 0:
            go(start=[0])
            kvq[1].fetch()
            kvq[2].fetch()
    for item in order:
        item.fetch()
    lat.spread()
    go(start=[1])
    go(spread=[0])
    lat.close()
    go(start=[2])
    go(spread=[1])
    for copy in token_copies:
        copy.wait_recv()

    reduce_copies, gather_copies, forward_copies = [], [], []

    def reduce_start(j):
        copies = []
        for place, (peer, chip) in enumerate(zip(spot.peers, spot.chips)):
            theirs = chip_block(chip)
            copies.append(net.remote(parts_ref.at[j, theirs], got_ref.at[j, place], peer))
            copies.append(net.remote(stat_ref.at[j, :, theirs], got_stat.at[j, place], peer))
        for copy in copies:
            copy.start()
        reduce_copies.append(copies)

    def combine(j):
        for copy in reduce_copies[j]:
            copy.wait_recv()
        mine = chip_block(spot.chip)
        stats = [stat_ref[j, :, mine]] + [got_stat[j, i] for i in range(3)]
        parts = [parts_ref[j, mine]] + [got_ref[j, i] for i in range(3)]
        best = functools.reduce(jnp.maximum, stats)
        rescale = [jnp.exp2(item - best) for item in stats]
        totals = [pltpu.roll(item, item.shape[0] - 2, 0) for item in stats]
        bottom = sum(a * b for a, b in zip(rescale, totals))
        table = [item / bottom for item in rescale]
        table.append(jnp.zeros((LANES - 8 * len(table), chip_rows), F32))
        table = jnp.concatenate(table, axis=0).T
        low = low_half((chip_rows, LANES))
        mixed = jnp.zeros((chip_rows, LANES), F32)
        for i, part in enumerate(parts):
            factor = jnp.where(low, table[:, 8 * i : 8 * i + 1], table[:, 8 * i + 1 : 8 * i + 2])
            mixed += part.astype(F32) * factor
        mix_all[mine, cols(j)] = mixed.astype(BF16)
        block = mix_all.at[mine, cols(j)]
        copies = [net.remote(block, block, to) for to in spot.peers + [spot.partner]]
        for copy in copies:
            copy.start()
        gather_copies.append(copies)

    def forward(j):
        copies = []
        for i, chip in enumerate(spot.chips):
            gather_copies[j][i].wait_recv()
            block = mix_all.at[chip_block(chip), cols(j)]
            copies.append(net.remote(block, block, spot.partner))
            copies[-1].start()
        forward_copies.append(copies)

    def forward_need(j):
        gather_copies[j][3].wait_recv()
        for copy in forward_copies[j]:
            copy.wait_recv()

    read_gain = [
        head_gain(scale_ref, 0, spot.core * heads + 2 * j, 2, head_dim) for j in range(blocks)
    ]
    early = [([2], [3]), ([3], [5]), ([5], [7])]
    after = [([], [4]), ([4], [6]), ([6], [])]
    for j in range(blocks):
        kvq[j].need()

        def key_rows(here):
            both = dot(norm_ref[here, :], kvq_ref[j, :, : 2 * LANES])
            k_ref[here, :] = unit_norm(both[:, :LANES], group)
            va_ref[here, :] = with_ones(both[:, LANES:])

        by_rows(2 * slab, 1024, key_rows)
        if j == 0:
            lat.need()
            in_ref[...] = rms(lat_all[...].astype(F32)).astype(BF16)
        q_ref[...] = unit_norm(dot(in_ref[...], kvq_ref[j, :, 2 * LANES :]), group, read_gain[j])
        if j >= 2:
            forward(j - 2)
        go(*early[j])
        tops, sums = two_heads(
            q_ref[...], k_ref[...], [va_ref[:, :LANES], va_ref[:, LANES:]], wide_a, wide_b, masks
        )
        low = low_half(sums[0].shape)
        parts_ref[j] = jnp.where(low, sums[0], sums[1]).astype(BF16)
        lane = lax.broadcasted_iota(jnp.int32, sums[0].shape, 1)
        stat = jnp.where(lane == 2, pltpu.roll(sums[0], LANES // 2, 1), sums[1])
        stat = jnp.where(lane == 0, tops[0], jnp.where(lane == 1, tops[1], stat))
        stat_ref[j] = stat.T[:8]
        reduce_start(j)
        if j >= 1:
            combine(j - 1)
        go(*after[j])

    write_gain = head_gain(scale_ref, 2, spot.core * heads, heads, head_dim)
    l4.need()

    def write_query_rows(here):
        wq_ref[here, :] = unit_norm(dot(norm_ref[here, :], w4_ref[...]), group, write_gain)

    by_rows(2 * slab, 1024, write_query_rows)
    r3.settle()
    forward(blocks - 2)
    combine(blocks - 1)
    go([7], [8, 9])
    forward(blocks - 1)
    r3.need()
    for j in range(blocks):
        forward_need(j)
    one_ref[...] = lat_all[...].astype(F32) + dot(mix_all[...], full_ref[0])
    in_ref[...] = rms(one_ref[...]).astype(BF16)
    l0.need()
    sq_ref[...] = unit_norm(
        dot(in_ref[...], wself_ref[:, :half]), group,
        head_gain(scale_ref, 1, spot.core * heads, heads, head_dim),
    )
    go([8])
    l1.need()
    sk_ref[...] = unit_norm(dot(in_ref[...], wself_ref[:, half : 2 * half]), group)
    go(start=[10])
    l2.need()
    sva_ref[...] = with_ones(dot(in_ref[...], wself_ref[:, 2 * half :]))

    go([9], [11])
    att_copies = [
        net.remote(att_ref.at[:, cols(j)], att_ref.at[:, cols(j)], spot.partner)
        for j in range(blocks)
    ]

    def span(start, size=LANES):
        return pl.ds(pl.multiple_of(start, LANES), size)

    def self_step(j, carry):
        for when in range(1, blocks):
            pl.when(j == when)(att_copies[when - 1].start)
        pl.when(j == blocks - 1)(l3.settle)
        here = span(j * LANES)
        _, sums = two_heads(
            sq_ref[:, here], sk_ref[:, here],
            [sva_ref[:, span((2 * j + i) * LANES)] for i in range(2)],
            tall_a.at[:rows], tall_b.at[:rows], masks,
        )
        att_ref[:, cols(j)] = quotient(sums)
        return carry

    lax.fori_loop(0, blocks, self_step, 0)
    att_copies[-1].start()
    go([10])
    l3.need()
    for copy in att_copies:
        copy.wait_recv()
    one_ref[...] = one_ref[...] + dot(att_ref[...], full_ref[1])
    lat_out_ref[...] = one_ref[pl.ds(pl.multiple_of(spot.me * own, own), own), :]
    in_ref[...] = rms(one_ref[...]).astype(BF16)
    go([11])
    l5.need()
    wk_ref[...] = unit_norm(dot(in_ref[...], wkv_ref[:, :half]), group)

    mix_copies = [
        net.remote(mix_ref.at[0, :, cols(j)], mix_ref.at[1, :, cols(j)], spot.partner)
        for j in range(blocks)
    ]
    steps = 2 * blocks

    def write_scores(index, head):
        part = index // blocks
        here = span((index % blocks) * LANES)
        queries = wq_ref[pl.ds(pl.multiple_of((1 - part) * slab, slab), slab), here]
        return inner(queries * masks[head], wk_ref[:, here])

    def powers(scores_ref):
        scores = scores_ref[...]
        return jnp.exp2(scores - jnp.max(scores, axis=1, keepdims=True)).astype(BF16)

    def score_step(index, carry):
        tall_b[...] = write_scores(index, 1)
        power_ref[index, 0] = powers(tall_a)
        tall_a[...] = write_scores((index + 1) % steps, 0)
        power_ref[index, 1] = powers(tall_b)
        return carry

    tall_a[...] = write_scores(0, 0)
    lax.fori_loop(0, steps, score_step, 0)
    l6.need()
    wva_ref[...] = with_ones(dot(in_ref[...], wkv_ref[:, half:]))

    for index in range(steps):
        if 1 <= index <= blocks:
            mix_copies[index - 1].start()
        part, j = index // blocks, index % blocks
        sums = [
            dot(power_ref[index, i], wva_ref[:, (2 * j + i) * LANES : (2 * j + i + 1) * LANES])
            for i in range(2)
        ]
        mix_ref[part, :, cols(j)] = quotient(sums)

    l7.need()
    for copy in mix_copies:
        copy.wait_recv()

    def out_rows(here):
        out_ref[here, :] = (
            tok_ref[here, :].astype(F32) + dot(mix_ref[1, here, :], full_ref[2])
        ).astype(out_ref.dtype)

    by_rows(slab, 1024, out_rows)
    for copy in net.sent:
        copy.wait_send()


def cube(count, tokens, latents, read_weights, later_weights, head_scale):
    own, width = latents.shape
    rows = own * count
    slab = tokens.shape[0]
    half = width // 2
    blocks = half // LANES
    vmem = lambda *shape: pltpu.VMEM(shape, BF16)
    full = lambda *shape: pltpu.VMEM(shape, F32)
    return pl.pallas_call(
        functools.partial(whole_body, count),
        out_shape=[
            jax.ShapeDtypeStruct(tokens.shape, BF16),
            jax.ShapeDtypeStruct(latents.shape, F32),
        ],
        in_specs=[VM, VM, pl.BlockSpec(memory_space=pl.ANY), pl.BlockSpec(memory_space=pl.ANY), SM],
        out_specs=[VM, VM],
        scratch_shapes=[
            vmem(2 * slab, width),
            vmem(blocks, width, 3 * LANES),
            vmem(width, half),
            vmem(width, 3 * half),
            vmem(width, 2 * half),
            vmem(3, width, width),
            vmem(rows, width),
            vmem(rows, LANES),
            vmem(2 * slab, LANES),
            vmem(2 * slab, 2 * LANES),
            full(rows, 2 * slab),
            full(rows, 2 * slab),
            full(slab, rows),
            full(slab, rows),
            vmem(blocks, rows, LANES),
            full(blocks, 8, rows),
            vmem(blocks, 3, 2 * own, LANES),
            full(blocks, 3, 8, 2 * own),
            vmem(rows, width),
            full(rows, width),
            vmem(rows, width),
            vmem(rows, half),
            vmem(rows, half),
            vmem(rows, 2 * half),
            vmem(rows, width),
            vmem(2 * slab, half),
            vmem(rows, half),
            vmem(rows, 2 * half),
            vmem(2, slab, width),
            vmem(2 * blocks, 2, slab, rows),
            pltpu.SemaphoreType.DMA((320,)),
            pltpu.SemaphoreType.DMA((320,)),
        ],
        compiler_params=pltpu.CompilerParams(
            vmem_limit_bytes=60 * 1024 * 1024, collective_id=0, has_side_effects=True
        ),
    )(tokens, latents, read_weights, later_weights, head_scale)


def solution(mesh):
    placed = (
        P(("vid", "seq"), None),
        P(("vid", "seq"), None),
        P(None, "seq", None),
        P(None, "seq", None),
        P(),
    )
    count = mesh.shape["seq"]
    form = cube if count == 2**3 and mesh.shape["vid"] % 2 == 0 else gathered
    return jax.shard_map(
        functools.partial(form, count),
        mesh=mesh,
        in_specs=placed,
        out_specs=(P(("vid", "seq"), None), P(("vid", "seq"), None)),
        check_vma=False,
    )
```

time: 129 us -> 85.5 us (0.66)
  Pallas kernels: 124 us -> 80.2 us
    pallas_call x1, Pallas kernels: 124 us -> 80.2 us  [cube(): pl.pallas_call(functools.partial(whole_body, count), out_shape=[jax.Shape...]
where the time goes in v1:
time: 85.5 us; the launch traced here: 84.3 us
  Pallas kernels  80.2 us (94%)
  local copies, waits for them, and re-layouts  3.37 us (4%)
    pallas_call x1, Pallas kernels, cube(): pl.pallas_call(functools.partial(whole_body, count), out_shape=[jax.Shape...  80.2 us
    unnamed x4, local copies, waits for them, and re-layouts  3.37 us

profile of v1, /device:TPU:1, one launch (start us, length us, event | category | flops | bytes accessed | tf_op | source)
XLA Modules:
  0.0 84.3 jit_solution(1642045710625028513)
XLA Ops:
  0.6 80.2 %shard_map.68 = (bf16[1024,768]{1,0:T(8,128)(2,1)}, f32[64,768]{1,0:T(8,128)}) custom-call(bf16[1024,768]{1,0:T(8,128)(2,1)} %tok_ref.1, bf16[64,768]{1,0:T(8,128)(2,1)} %lat_ref.1, bf16[4,96,768]{2,1,0:T(8,128)(2,1)} %rw_ref.1, bf16[8,96,768]{2,1,0:T(8,128)(2,1)} %lw_ref.1, f32[3,12]{1,0:T(4,128)} %scale_ref.1), custom_call_target="tpu_custom_call" | custom-call | tf_op jit(solution)/shard_map/pallas_call | solution.py:819
  80.9 0.0 copy-start
  80.9 2.7 %copy.9 = bf16[1024,768]{1,0:T(8,128)(2,1)} copy(bf16[1024,768]{1,0:T(8,128)(2,1)} %get-tuple-element.4) | data formatting | bytes 3145728
  83.6 0.0 copy-done
  83.6 0.7 copy.10
Async XLA Ops:
  80.9 2.7 %copy-start = (f32[64,768]{1,0:T(8,128)S(1)}, f32[64,768]{1,0:T(8,128)}, u32[]{:S(2)}) copy-start(f32[64,768]{1,0:T(8,128)} %get-tuple-element.5) | copy-start | bytes 589828
